TPU v7x, 32 devices: a whole 2x2x4 slice. The times are simulated.
32 devices in a mesh: row: 4 (over x, core), col: 8 (over z, y).
Axes of the slice: x: 2, y: 2, z: 4, core: 2. Of those that a mesh axis runs over, the one named last changes fastest.
Arguments:
- tokens: bfloat16 [128, 12288], P('col', 'row'), may hold values from -6 to 6
- w_in: bfloat16 [12288, 24576], P('row', 'col'), may hold values from -0.078125 to 0.078125
- w_out: bfloat16 [24576, 12288], P('col', 'row'), may hold values from -0.0546875 to 0.0546875
- mask_in: int32 [96, 192], P('row', 'col'), may hold values 0 or 1
- mask_out: int32 [192, 96], P('col', 'row'), may hold values 0 or 1
- out_grad: bfloat16 [128, 12288], P('col', 'row'), may hold values from -1.5 to 1.5
Outputs:
- mixed: bfloat16 [128, 12288], P('col', 'row')
- tokens_grad: bfloat16 [128, 12288], P('col', 'row')
- w_in_grad: bfloat16 [12288, 24576], P('row', 'col')
- w_out_grad: bfloat16 [24576, 12288], P('col', 'row')
Inputs may be any that keep to these rules, and one draw needn't show every extreme that they name: `mask_in`: one flag per block. `mask_out`: one flag per block.
All inputs are finite; a program needn't handle non-finite values.
Results may differ from a plain program's by a relative error of at most 0.0049.
Values may be sent and summed in bfloat16 or wider, within the bound.
A program may use at most 192 MiB of HBM per device.

v0:
```python
import functools
import math

import jax
import jax.numpy as jnp
from jax import lax
from jax.experimental import pallas as pl
from jax.experimental.pallas import tpu as pltpu
from jax.sharding import PartitionSpec as P

BLK = 128
SUB = 16
MESH = pl.DeviceIdType.MESH
VMEM = pl.BlockSpec(memory_space=pltpu.VMEM)
DMA = pltpu.SemaphoreType.DMA
GELU_A, GELU_B = 0.7978845608028654, 0.044715


def remote(src, dst, send, recv, axis, device):
    return pltpu.make_async_remote_copy(
        src_ref=src, dst_ref=dst, send_sem=send, recv_sem=recv,
        device_id={axis: device}, device_id_type=MESH,
    )


def greet(axis, peers):
    barrier = pltpu.get_barrier_semaphore()
    for peer in peers:
        pl.semaphore_signal(barrier, inc=1, device_id={axis: peer}, device_id_type=MESH)
    pl.semaphore_wait(barrier, len(peers))


def spread(mask):
    rows, cols = mask.shape

    def repeats(shape, dim, size):
        apart = lax.broadcasted_iota(jnp.int32, shape, dim) - size * lax.broadcasted_iota(jnp.int32, shape, 1 - dim)
        return jnp.where((apart >= 0) & (apart < size), 1.0, 0.0).astype(jnp.bfloat16)

    flags = mask.astype(jnp.float32).astype(jnp.bfloat16)
    tall = jnp.dot(repeats((rows * SUB, rows), 0, SUB), flags, preferred_element_type=jnp.float32)
    wide = jnp.dot(tall.astype(jnp.bfloat16), repeats((cols, cols * BLK), 1, BLK), preferred_element_type=jnp.float32)
    return wide.astype(jnp.bfloat16)


def masked(weight, flags):
    rows, cols = weight.shape
    shaped = weight.reshape(rows // BLK, BLK // SUB, SUB, cols)
    return (shaped * flags.reshape(rows // BLK, 1, SUB, cols)).reshape(rows, cols)


def tiling(width):
    tile = 2 * BLK if width % (2 * BLK) == 0 else BLK
    tiles = width // tile
    pieces = next(count for count in (4, 3, 2, 1) if tiles % count == 0)
    return tile, tiles, pieces


def stream_shapes(depth, tile):
    return [
        pltpu.VMEM((2, depth, tile), jnp.bfloat16), pltpu.VMEM((2, depth // BLK * SUB, tile), jnp.bfloat16),
        pltpu.VMEM((2, tile, depth), jnp.bfloat16), pltpu.VMEM((2, tile // BLK * SUB, depth), jnp.bfloat16),
        DMA((4, 2)),
    ]


def streamed(tile, tiles, left, right, sources, buffers):
    *slots, arrived = buffers
    rows = tile // BLK * SUB

    def copies(t):
        slot = lax.rem(t, 2)
        across = pl.ds(pl.multiple_of(t * tile, tile), tile)
        down = pl.ds(pl.multiple_of(t * rows, rows), rows)
        views = [sources[0].at[:, across], sources[1].at[:, across], sources[2].at[across, :], sources[3].at[down, :]]
        return [pltpu.make_async_copy(view, slots[n].at[slot], arrived.at[n, slot]) for n, view in enumerate(views)]

    def first():
        for copy in copies(0):
            copy.start()

    def pair(t):
        for copy in copies(t):
            copy.wait()

        @pl.when(t + 1 < tiles)
        def _():
            for copy in copies(t + 1):
                copy.start()

        slot = lax.rem(t, 2)
        ahead = jnp.dot(left[...], masked(slots[0][slot], slots[1][slot]), preferred_element_type=jnp.float32)
        back = lax.dot_general(
            right[...], masked(slots[2][slot], slots[3][slot]),
            (((1,), (1,)), ((), ())), preferred_element_type=jnp.float32,
        )
        return ahead, back

    return first, pair


def gelu_parts(value):
    square = value * value
    tanh = jnp.tanh(GELU_A * (value + GELU_B * (square * value)))
    half = 0.5 * (1.0 + tanh)
    slope = half + 0.5 * value * (1.0 - tanh * tanh) * (GELU_A * (1.0 + (3.0 * GELU_B) * square))
    return value * half, slope


def front_kernel(far, near, chips, cores, tile, tiles, pieces, *refs):
    srcs, masks, weights, outs, dsts, flags = (refs[n:n + 2] for n in range(0, 12, 2))
    down_slots, up_slots, arrived, zs, zr, ys, yr, own = refs[12:20]
    parts, pair, sums, landed, slopes, ps, pr, xs, xr, gs, gr, fs, fr = refs[20:]
    slots = (down_slots, up_slots)
    mine = lax.axis_index("col")
    z, y = mine // near, lax.rem(mine, near)
    along_z = [lax.rem(z + d, far) * near + y for d in range(1, far)]
    along_y = [z * near + lax.rem(y + e, near) for e in range(1, near)]
    me = lax.axis_index("row")
    x, k = me // cores, lax.rem(me, cores)
    partner = x * cores + (1 - k)
    across = [lax.rem(x + d, chips) for d in range(1, chips)]
    peers = [c * cores + k for c in across]
    per = tiles // pieces
    cols = per * tile
    shaped = parts.shape[2:5]
    rows = tile // BLK * SUB
    sent = []

    def push(copy):
        copy.start()
        sent.append(copy)

    def fetch(a, t):
        slot = lax.rem(t, 2)
        spot = pl.ds(pl.multiple_of(t * tile, tile), tile)
        view = weights[0].at[:, spot] if a == 0 else weights[1].at[spot, :]
        return pltpu.make_async_copy(view, slots[a].at[slot], arrived.at[a, slot])

    for a in range(2):
        fetch(a, jnp.int32(0)).start()
    barrier = pltpu.get_barrier_semaphore()
    for axis, group in (("col", along_z + along_y), ("row", [partner] + peers)):
        for peer in group:
            pl.semaphore_signal(barrier, inc=1, device_id={axis: peer}, device_id_type=MESH)
    pl.semaphore_wait(barrier, len(along_z) + len(along_y) + len(peers) + 1)

    def give(a):
        for e, peer in enumerate(along_y):
            push(remote(srcs[a], dsts[a].at[mine], ys.at[a, 0, e], yr.at[a, 0, e], "col", peer))
        for d, peer in enumerate(along_z):
            push(remote(srcs[a], dsts[a].at[mine], zs.at[a, d], zr.at[a, d], "col", peer))

    give(0)
    kept = [pltpu.make_async_copy(srcs[a], dsts[a].at[mine], own.at[a]) for a in range(2)]
    for copy in kept:
        copy.start()
    for a in range(2):
        flags[a][...] = spread(masks[a][...])

    def relay(a, d):
        slot = dsts[a].at[lax.rem(z + far - d - 1, far) * near + y]
        remote(srcs[a], slot, zs.at[a, d], zr.at[a, d], "col", along_z[d]).wait_recv()
        for e, peer in enumerate(along_y):
            push(remote(slot, slot, ys.at[a, d + 1, e], yr.at[a, d + 1, e], "col", peer))

    def gathered(a):
        for d in range(far):
            for e in range(near - 1):
                slot = dsts[a].at[lax.rem(z + far - d, far) * near + lax.rem(y + near - e - 1, near)]
                remote(slot, slot, ys.at[a, d, e], yr.at[a, d, e], "col", along_y[e]).wait_recv()
        kept[a].wait()

    def to_partner(a, p):
        return remote(parts.at[a, p, :, 1 - k], pair.at[a, p], ps.at[a, p], pr.at[a, p], "row", partner)

    def to_chip(a, p, d):
        return remote(sums.at[a, p, d], landed.at[a, p, d], xs.at[a, p, d], xr.at[a, p, d], "row", peers[d])

    def share(a, p, owner):
        return outs[a].at[owner, :, pl.ds(p * cols, cols)]

    def give_chip(a, p, d, owner):
        return remote(share(a, p, owner), share(a, p, owner), gs.at[a, p, d], gr.at[a, p, d], "row", peers[d])

    def give_partner(a, p, d, owner):
        return remote(share(a, p, owner), share(a, p, owner), fs.at[a, p, d], fr.at[a, p, d], "row", partner)

    def compute(a, p):
        if p == 0:
            gathered(a)

        def step(j, carry):
            t = p * per + j
            slot = lax.rem(t, 2)
            fetch(a, t).wait()

            @pl.when(t + 1 < tiles)
            def _():
                fetch(a, t + 1).start()

            left = dsts[a][...].reshape(-1, dsts[a].shape[-1])
            if a == 0:
                marks = flags[0][:, pl.ds(pl.multiple_of(t * tile, tile), tile)]
            else:
                marks = flags[1][pl.ds(pl.multiple_of(t * rows, rows), rows), :]
            value = lax.dot_general(
                left, masked(slots[a][slot], marks), (((1,), (a,)), ((), ())), preferred_element_type=jnp.float32
            )
            parts[a, p, :, :, :, pl.ds(pl.multiple_of(j * tile, tile), tile)] = value.reshape(*shaped, tile)
            return carry

        lax.fori_loop(0, per, step, 0)
        push(to_partner(a, p))
        if a == 0:
            for d in range(far - 1):
                if d * pieces // (far - 1) == p:
                    relay(1, d)

    def reduce_pair(a, p):
        to_partner(a, p).wait_recv()
        for d, c in enumerate(across):
            sums[a, p, d] = (parts[a, p, c, k] + pair[a, p, c]).astype(sums.dtype)
            push(to_chip(a, p, d))

    def finish(a, p):
        total = parts[a, p, x, k] + pair[a, p, x]
        for d in range(chips - 1):
            to_chip(a, p, d).wait_recv()
            total = total + landed[a, p, d].astype(jnp.float32)
        if a == 0:
            value, slopes[p] = gelu_parts(total)
        else:
            value = total * slopes[p]
        outs[a][me, :, pl.ds(p * cols, cols)] = value.astype(outs[a].dtype)
        for d in range(chips - 1):
            push(give_chip(a, p, d, me))
        push(give_partner(a, p, chips - 1, me))

    def forward(a, p):
        for d in range(chips - 1):
            owner = lax.rem(x + chips - d - 1, chips) * cores + k
            give_chip(a, p, d, owner).wait_recv()
            push(give_partner(a, p, d, owner))

    for d in range(far - 1):
        relay(0, d)
    give(1)
    stages = (compute, reduce_pair, finish, forward)
    jobs = [(a, p) for a in range(2) for p in range(pieces)]
    for step in range(len(jobs) + len(stages) - 1):
        for lag, stage in enumerate(stages):
            if 0 <= step - lag < len(jobs):
                stage(*jobs[step - lag])
    for a, p in jobs:
        for d in range(chips):
            owner = lax.rem(x + chips - lax.rem(d + 1, chips), chips) * cores + (1 - k)
            give_partner(a, p, d, owner).wait_recv()
    for copy in sent:
        copy.wait_send()


ANY = pl.BlockSpec(memory_space=pl.ANY)


def front_stage(far, near, chips, cores, first, second, masks, down, up):
    depth, width = down.shape
    tokens = first.shape[0] * far * near
    tile, tiles, pieces = tiling(width)
    cols = width // pieces
    share = tokens // (chips * cores)
    out = jax.ShapeDtypeStruct((chips * cores, share, width), jnp.bfloat16)
    full = jax.ShapeDtypeStruct((far * near,) + first.shape, first.dtype)
    spreads = tuple(
        jax.ShapeDtypeStruct((each.shape[0] * SUB, each.shape[1] * BLK), jnp.bfloat16) for each in masks
    )
    act, hid, gathered, grad_rows, in_flags, out_flags = pl.pallas_call(
        functools.partial(front_kernel, far, near, chips, cores, tile, tiles, pieces),
        out_shape=(out, out, full, full) + spreads,
        in_specs=[VMEM] * 4 + [ANY] * 2,
        out_specs=(VMEM,) * 6,
        scratch_shapes=[
            pltpu.VMEM((2, depth, tile), jnp.bfloat16), pltpu.VMEM((2, tile, depth), jnp.bfloat16), DMA((2, 2)),
            DMA((2, far - 1)), DMA((2, far - 1)),
            DMA((2, far, near - 1)), DMA((2, far, near - 1)), DMA((2,)),
            pltpu.VMEM((2, pieces, chips, cores, share, cols), jnp.float32),
            pltpu.VMEM((2, pieces, chips, share, cols), jnp.float32),
            pltpu.VMEM((2, pieces, chips - 1, share, cols), jnp.bfloat16),
            pltpu.VMEM((2, pieces, chips - 1, share, cols), jnp.bfloat16),
            pltpu.VMEM((pieces, share, cols), jnp.float32),
            DMA((2, pieces)), DMA((2, pieces)),
            DMA((2, pieces, chips - 1)), DMA((2, pieces, chips - 1)),
            DMA((2, pieces, chips - 1)), DMA((2, pieces, chips - 1)),
            DMA((2, pieces, chips)), DMA((2, pieces, chips)),
        ],
        compiler_params=pltpu.CompilerParams(collective_id=0, has_side_effects=True),
        name="front_stage",
    )(first, second, *masks, down, up)
    flat = lambda each: each.reshape(tokens, each.shape[-1])
    return flat(act), flat(hid), flat(gathered), flat(grad_rows), in_flags, out_flags


def column_kernel(far, near, tile, tiles, pieces, left, right, *refs):
    sources, outs, refs = refs[:4], refs[4:6], refs[6:]
    buffers, refs = refs[:5], refs[5:]
    wide, short, across, sums, landed, ys, yr, zs, zr = refs
    me = lax.axis_index("col")
    z, y = me // near, lax.rem(me, near)
    rows_y = [lax.rem(y + e, near) for e in range(1, near)]
    rows_z = [lax.rem(z + d, far) for d in range(1, far)]
    peers_y = [z * near + e for e in rows_y]
    peers_z = [d * near + y for d in rows_z]
    first, multiply = streamed(tile, tiles, left, right, sources, buffers)
    first()
    greet("col", peers_y + peers_z)
    per = tiles // pieces
    cols = per * tile
    shaped = wide.shape[2:5]
    sent = []

    def push(copy):
        copy.start()
        sent.append(copy)

    def over_y(a, p, e):
        return remote(short.at[a, p, :, rows_y[e]], across.at[a, p, e], ys.at[a, p, e], yr.at[a, p, e], "col", peers_y[e])

    def over_z(a, p, d):
        return remote(sums.at[a, p, d], landed.at[a, p, d], zs.at[a, p, d], zr.at[a, p, d], "col", peers_z[d])

    def near_sum(a, p, row):
        total = wide[a, p, row, y]
        for e in range(near - 1):
            total = total + across[a, p, e, row].astype(jnp.float32)
        return total

    def compute(p):
        def step(j, carry):
            spot = pl.ds(pl.multiple_of(j * tile, tile), tile)
            for a, value in enumerate(multiply(p * per + j)):
                laid = value.reshape(*shaped, tile)
                wide[a, p, :, :, :, spot] = laid
                short[a, p, :, :, :, spot] = laid.astype(short.dtype)
            return carry

        lax.fori_loop(0, per, step, 0)
        for a in range(2):
            for e in range(near - 1):
                push(over_y(a, p, e))

    def reduce_near(p):
        for a in range(2):
            for e in range(near - 1):
                over_y(a, p, e).wait_recv()
            for d in range(far - 1):
                sums[a, p, d] = near_sum(a, p, rows_z[d]).astype(sums.dtype)
                push(over_z(a, p, d))

    def finish(p):
        for a in range(2):
            total = near_sum(a, p, z)
            for d in range(far - 1):
                over_z(a, p, d).wait_recv()
                total = total + landed[a, p, d].astype(jnp.float32)
            outs[a][:, pl.ds(p * cols, cols)] = total.astype(outs[a].dtype)

    stages = (compute, reduce_near, finish)
    for step in range(pieces + len(stages) - 1):
        for lag, stage in enumerate(stages):
            if 0 <= step - lag < pieces:
                stage(step - lag)
    for copy in sent:
        copy.wait_send()


def column_stage(far, near, left, right, down, down_flags, up, up_flags):
    tokens, depth = left.shape
    width = down.shape[1]
    tile, tiles, pieces = tiling(width)
    cols = width // pieces
    share = tokens // (far * near)
    out = jax.ShapeDtypeStruct((share, width), jnp.bfloat16)
    return pl.pallas_call(
        functools.partial(column_kernel, far, near, tile, tiles, pieces),
        out_shape=(out, out),
        in_specs=[VMEM] * 2 + [ANY] * 4,
        out_specs=(VMEM, VMEM),
        scratch_shapes=stream_shapes(depth, tile) + [
            pltpu.VMEM((2, pieces, far, near, share, cols), jnp.float32),
            pltpu.VMEM((2, pieces, far, near, share, cols), jnp.bfloat16),
            pltpu.VMEM((2, pieces, near - 1, far, share, cols), jnp.bfloat16),
            pltpu.VMEM((2, pieces, far - 1, share, cols), jnp.bfloat16),
            pltpu.VMEM((2, pieces, far - 1, share, cols), jnp.bfloat16),
            DMA((2, pieces, near - 1)), DMA((2, pieces, near - 1)),
            DMA((2, pieces, far - 1)), DMA((2, pieces, far - 1)),
        ],
        compiler_params=pltpu.CompilerParams(collective_id=2, has_side_effects=True),
        name="column_stage",
    )(left, right, down, down_flags, up, up_flags)


def outer_kernel(tokens_ref, hid_ref, in_flags, act_ref, grad_ref, out_flags, in_ref, out_ref):
    def one(left, right, flags, out):
        full = lax.dot_general(left, right, (((0,), (0,)), ((), ())), preferred_element_type=jnp.float32)
        out[...] = masked(full.astype(out.dtype), flags)

    one(tokens_ref[...], hid_ref[...], in_flags[...], in_ref)
    one(act_ref[...], grad_ref[...], out_flags[...], out_ref)


def outers(tokens, hid, in_flags, act, grad, out_flags):
    count, depth = tokens.shape
    width = hid.shape[1]
    steps = math.gcd(depth // BLK, width // BLK)
    steps = steps // 2 if steps % 2 == 0 else steps
    down, up = depth // steps, width // steps
    whole = lambda each: pl.BlockSpec(each.shape, lambda i: (0, 0))
    return pl.pallas_call(
        outer_kernel,
        grid=(steps,),
        out_shape=[
            jax.ShapeDtypeStruct((depth, width), jnp.bfloat16),
            jax.ShapeDtypeStruct((width, depth), jnp.bfloat16),
        ],
        in_specs=[
            pl.BlockSpec((count, down), lambda i: (0, i)), whole(hid),
            pl.BlockSpec((down // BLK * SUB, width), lambda i: (i, 0)),
            pl.BlockSpec((count, up), lambda i: (0, i)), whole(grad),
            pl.BlockSpec((up // BLK * SUB, depth), lambda i: (i, 0)),
        ],
        out_specs=[
            pl.BlockSpec((down, width), lambda i: (i, 0)),
            pl.BlockSpec((up, depth), lambda i: (i, 0)),
        ],
        name="outers",
    )(tokens, hid, in_flags, act, grad, out_flags)


def local(far, near, chips, cores, tokens, w_in, w_out, mask_in, mask_out, out_grad):
    act, hid, gathered, grad_rows, in_flags, out_flags = front_stage(
        far, near, chips, cores, tokens, out_grad, (mask_in, mask_out), w_in, w_out
    )
    mixed, tokens_grad = column_stage(far, near, act, hid, w_out, out_flags, w_in, in_flags)
    w_in_grad, w_out_grad = outers(gathered, hid, in_flags, act, grad_rows, out_flags)
    return (mixed, tokens_grad, w_in_grad, w_out_grad)


def solution(mesh):
    columns, rows = mesh.shape["col"], mesh.shape["row"]
    near = 2 ** (int(math.log2(columns)) // 2)
    return jax.shard_map(
        functools.partial(local, columns // near, near, rows // 2, 2),
        mesh=mesh,
        in_specs=(
            P("col", "row"),
            P("row", "col"),
            P("col", "row"),
            P("row", "col"),
            P("col", "row"),
            P("col", "row"),
        ),
        out_specs=(P("col", "row"), P("col", "row"), P("row", "col"), P("col", "row")),
        check_vma=False,
    )
```

profile of v0, /device:TPU:0, one launch (start us, length us, event | category | flops | bytes accessed | tf_op | source)
XLA Modules:
  0.0 126.6 jit_solution(7467155622784914418)
XLA Ops:
  0.6 65.9 %front_stage.1 = (bf16[4,32,3072]{2,1,0:T(8,128)(2,1)}, bf16[4,32,3072]{2,1,0:T(8,128)(2,1)}, bf16[8,16,3072]{2,1,0:T(8,128)(2,1)}, bf16[8,16,3072]{2,1,0:T(8,12...) custom-call(bf16[16,3072]{1,0:T(8,128)(2,1)} %refs_0_.2, bf16[16,3072]{1,0:T(8,128)(2,1)} %refs_1_.1, ...), custom_call_target="tpu_custom_call" | custom-call | tf_op jit(solution)/shard_map/front_stage/pallas_call | solution.py:277
  66.5 18.3 %outers.1 = (bf16[3072,3072]{1,0:T(8,128)(2,1)}, bf16[3072,3072]{1,0:T(8,128)(2,1)}) custom-call(bf16[128,3072]{1,0:T(8,128)(2,1)} %bitcast.8, bf16[128,3072]{1,0:T(8,128)(2,1)} %bitcast.6, bf16[384,3072]{1,0:T(8,128)(2,1)} %get-tuple-element.17.refs_3_.in_flags, bf16[128,3072]{1,0:T(8,128)(2,1)} %bitcast.4, bf16[128,3072]{1,0:T(8,128)(2,1)} %bitcast.9, ...), custom_call_target="tpu_custom_call" | custom-call | tf_op jit(solution)/shard_map/outers/pallas_call | solution.py:418
  84.8 38.7 %column_stage.1 = (bf16[16,3072]{1,0:T(8,128)(2,1)}, bf16[16,3072]{1,0:T(8,128)(2,1)}) custom-call(bf16[128,3072]{1,0:T(8,128)(2,1)} %bitcast.5, bf16[128,3072]{1,0:T(8,128)(2,1)} %bitcast.7, bf16[3072,3072]{1,0:T(8,128)(2,1)} %refs_0_.3, bf16[384,3072]{1,0:T(8,128)(2,1)} %get-tuple-element.16.refs_1_.out_flags, bf16[3072,3072]{1,0:T(8,128)(2,1)} %refs_2_.3, ...), custom_call_target="tpu_custom_call" | custom-call | tf_op jit(solution)/shard_map/column_stage/pallas_call | solution.py:383
  123.5 1.5 %copy.12 = bf16[16,3072]{1,0:T(8,128)(2,1)} copy(bf16[16,3072]{1,0:T(8,128)(2,1)} %get-tuple-element.28) | data formatting | bytes 196608
  125.1 1.5 %copy.13 = bf16[16,3072]{1,0:T(8,128)(2,1)} copy(bf16[16,3072]{1,0:T(8,128)(2,1)} %get-tuple-element.29) | data formatting | bytes 196608
where the time goes:
time: 128 us; the launch traced here: 127 us
  Pallas kernels  123 us (96%)
  local copies, waits for them, and re-layouts  3.08 us (2%)
    pallas_call x1, Pallas kernels, front_stage(): pl.pallas_call(functools.partial(front_kernel, far, near, chips, cores, t...  65.9 us
    pallas_call x1, Pallas kernels, column_stage(): pl.pallas_call(functools.partial(column_kernel, far, near, tile, tiles, p...  38.7 us
    pallas_call x1, Pallas kernels, outers(): pl.pallas_call(outer_kernel, grid=(steps,), out_shape=[jax.ShapeDtypeStru...  18.3 us
    unnamed x2, local copies, waits for them, and re-layouts  3.08 us

commit v1 on v0

v1 whole, which is shorter than its diff:
```python
import functools
import math

import jax
import jax.numpy as jnp
from jax import lax
from jax.experimental import pallas as pl
from jax.experimental.pallas import tpu as pltpu
from jax.sharding import PartitionSpec as P

BLK = 128
SUB = 16
MESH = pl.DeviceIdType.MESH
VMEM = pl.BlockSpec(memory_space=pltpu.VMEM)
DMA = pltpu.SemaphoreType.DMA
COLS, SPAN, STEP = 512, 512, 512
GELU_A, GELU_B = 0.7978845608028654, 0.044715


def remote(src, dst, send, recv, axis, device):
    return pltpu.make_async_remote_copy(
        src_ref=src, dst_ref=dst, send_sem=send, recv_sem=recv,
        device_id={axis: device}, device_id_type=MESH,
    )


def spread(mask, start, count):
    rows, cols = mask.shape

    def repeats(shape, dim, size, offset):
        apart = lax.broadcasted_iota(jnp.int32, shape, dim) - size * (
            lax.broadcasted_iota(jnp.int32, shape, 1 - dim) - offset
        )
        return jnp.where((apart >= 0) & (apart < size), 1.0, 0.0).astype(jnp.bfloat16)

    flags = mask.astype(jnp.float32).astype(jnp.bfloat16)
    tall = jnp.dot(repeats((count * SUB, rows), 0, SUB, start), flags, preferred_element_type=jnp.float32)
    wide = jnp.dot(tall.astype(jnp.bfloat16), repeats((cols, cols * BLK), 1, BLK, 0), preferred_element_type=jnp.float32)
    return wide.astype(jnp.bfloat16)


def masked(weight, flags):
    rows, cols = weight.shape
    shaped = weight.reshape(rows // BLK, BLK // SUB, SUB, cols)
    return (shaped * flags.reshape(rows // BLK, 1, SUB, cols)).reshape(rows, cols)


def cut(width, most):
    return next(width // count for count in range(1, width // BLK + 1)
                if width % (count * BLK) == 0 and width // count <= most)


def gelu_parts(value):
    square = value * value
    tanh = jnp.tanh(GELU_A * (value + GELU_B * (square * value)))
    half = 0.5 * (1.0 + tanh)
    slope = half + 0.5 * value * (1.0 - tanh * tanh) * (GELU_A * (1.0 + (3.0 * GELU_B) * square))
    return value * half, slope


def layer_kernel(far, near, chips, cores, *refs):
    srcs, masks, weights = refs[:2], refs[2:4], refs[4:6]
    tokens_t, act_t, hid, grad_rows, mixed, tokens_grad = refs[6:12]
    flags, held, loaded, token_rows, act = refs[12:14], refs[14:16], refs[16:18], refs[18], refs[19]
    zs, zr, ys, yr, own = refs[20:25]
    parts, pair, sums, landed, slopes, ps, pr, xs, xr, gs, gr = refs[25:36]
    wide, short, over, near_sums, far_parts, cys, cyr, czs, czr = refs[36:]
    dsts, sides = (token_rows, grad_rows), (act, hid)
    results = (mixed, tokens_grad)
    mine = lax.axis_index("col")
    z, y = mine // near, lax.rem(mine, near)
    rows_z = [lax.rem(z + d, far) for d in range(1, far)]
    rows_y = [lax.rem(y + e, near) for e in range(1, near)]
    along_z = [r * near + y for r in rows_z]
    along_y = [z * near + r for r in rows_y]
    me = lax.axis_index("row")
    x, k = me // cores, lax.rem(me, cores)
    partner = x * cores + (1 - k)
    peers = [lax.rem(x + d, chips) * cores + k for d in range(1, chips)]
    pieces, cols = parts.shape[1], parts.shape[-1]
    chunks, span = wide.shape[1], wide.shape[-1]
    shaped = wide.shape[2:5]
    sent = []

    def push(copy):
        copy.start()
        sent.append(copy)

    def load(a, p):
        spot = pl.ds(p * cols, cols)
        if a == 0:
            return pltpu.make_async_copy(weights[0].at[:, spot], held[0].at[:, spot], loaded[0].at[p])
        return pltpu.make_async_copy(weights[1].at[spot, :], held[1].at[spot, :], loaded[1].at[p])

    for p in range(pieces):
        load(0, p).start()
    barrier = pltpu.get_barrier_semaphore()
    for axis, group in (("col", along_z + along_y), ("row", [partner] + peers)):
        for peer in group:
            pl.semaphore_signal(barrier, inc=1, device_id={axis: peer}, device_id_type=MESH)
    pl.semaphore_wait(barrier, len(along_z) + len(along_y) + len(peers) + 1)

    def give(a):
        for e, peer in enumerate(along_y):
            push(remote(srcs[a], dsts[a].at[mine], ys.at[a, 0, e], yr.at[a, 0, e], "col", peer))
        for d, peer in enumerate(along_z):
            push(remote(srcs[a], dsts[a].at[mine], zs.at[a, d], zr.at[a, d], "col", peer))

    def relay(a, d):
        slot = dsts[a].at[lax.rem(z + far - d - 1, far) * near + y]
        remote(srcs[a], slot, zs.at[a, d], zr.at[a, d], "col", along_z[d]).wait_recv()
        for e, peer in enumerate(along_y):
            push(remote(slot, slot, ys.at[a, d + 1, e], yr.at[a, d + 1, e], "col", peer))

    def gathered(a):
        for d in range(far):
            for e in range(near - 1):
                slot = dsts[a].at[lax.rem(z + far - d, far) * near + lax.rem(y + near - e - 1, near)]
                remote(slot, slot, ys.at[a, d, e], yr.at[a, d, e], "col", along_y[e]).wait_recv()
        kept[a].wait()

    def rows_of(ref):
        return ref[...].reshape(-1, ref.shape[-1])

    def ahead(left, a, start, size):
        spot = pl.ds(start, size)
        return jnp.dot(left, masked(held[a][:, spot], flags[a][:, spot]), preferred_element_type=jnp.float32)

    def back(right, a, start, size):
        spot, marks = pl.ds(start, size), pl.ds(start // BLK * SUB, size // BLK * SUB)
        turned = lax.dot_general(
            masked(held[a][spot, :], flags[a][marks, :]), right, (((1,), (1,)), ((), ())),
            preferred_element_type=jnp.float32,
        )
        return turned.T

    def to_partner(a, p):
        return remote(parts.at[a, p, 1 - k], pair.at[a, p], ps.at[a, p], pr.at[a, p], "row", partner)

    def to_chip(a, p, d):
        return remote(sums.at[a, p], landed.at[a, p, d], xs.at[a, p, d], xr.at[a, p, d], "row", peers[d])

    def give_partner(a, p, owner):
        share = sides[a].at[owner, :, pl.ds(p * cols, cols)]
        return remote(share, share, gs.at[a, p], gr.at[a, p], "row", partner)

    def compute(a, p):
        load(a, p).wait()
        value = (ahead if a == 0 else back)(rows_of(dsts[a]), a, p * cols, cols)
        parts[a, p] = value.reshape(parts.shape[2:])
        push(to_partner(a, p))

    def reduce_pair(a, p):
        to_partner(a, p).wait_recv()
        total = parts[a, p, k] + pair[a, p]
        pair[a, p] = total
        sums[a, p] = total.astype(sums.dtype)
        for d in range(chips - 1):
            push(to_chip(a, p, d))

    def finish(a, p):
        total = pair[a, p]
        for d in range(chips - 1):
            to_chip(a, p, d).wait_recv()
            total = total + landed[a, p, d].astype(jnp.float32)
        if a == 0:
            value, slopes[p] = gelu_parts(total)
        else:
            value = total * slopes[p]
        sides[a][k, :, pl.ds(p * cols, cols)] = value.astype(sides[a].dtype)
        push(give_partner(a, p, k))

    def arrive(a):
        for p in range(pieces):
            give_partner(a, p, 1 - k).wait_recv()

    def over_y(a, q, e):
        return remote(short.at[a, q, :, rows_y[e]], over.at[a, q, e], cys.at[a, q, e], cyr.at[a, q, e], "col", along_y[e])

    def over_z(a, q, d):
        return remote(near_sums.at[a, q, d], far_parts.at[a, q, d], czs.at[a, q, d], czr.at[a, q, d], "col", along_z[d])

    def near_sum(a, q, row):
        total = wide[a, q, row, y]
        for e in range(near - 1):
            total = total + over[a, q, e, row].astype(jnp.float32)
        return total

    def output(a, q):
        value = (ahead if a == 0 else back)(rows_of(sides[a]), 1 - a, q * span, span)
        laid = value.reshape(*shaped, span)
        wide[a, q] = laid
        short[a, q] = laid.astype(short.dtype)
        for e in range(near - 1):
            push(over_y(a, q, e))

    def reduce_near(a, q):
        for e in range(near - 1):
            over_y(a, q, e).wait_recv()
        for d in range(far - 1):
            near_sums[a, q, d] = near_sum(a, q, rows_z[d]).astype(near_sums.dtype)
            push(over_z(a, q, d))

    def settle(a, q):
        total = near_sum(a, q, z)
        for d in range(far - 1):
            over_z(a, q, d).wait_recv()
            total = total + far_parts[a, q, d].astype(jnp.float32)
        results[a][:, pl.ds(q * span, span)] = total.astype(results[a].dtype)

    give(0)
    kept = [pltpu.make_async_copy(srcs[a], dsts[a].at[mine], own.at[a]) for a in range(2)]
    for copy in kept:
        copy.start()
    for a in range(2):
        flags[a][...] = spread(masks[a][...], 0, masks[a].shape[0])
    for d in range(far - 1):
        relay(0, d)
    give(1)
    for p in range(pieces):
        load(1, p).start()
    gathered(0)

    def spaced(main, side):
        done = 0
        for n, job in enumerate(main):
            job()
            upto = (n + 1) * len(side) // len(main)
            for other in side[done:upto]:
                other()
            done = upto

    call = functools.partial
    relays = [call(relay, 1, d) for d in range(far - 1)]
    main = [call(compute, 0, 0)]
    for p in range(1, pieces):
        main += [call(compute, 0, p), call(reduce_pair, 0, p - 1)]
    main += [call(reduce_pair, 0, pieces - 1)]
    main += [call(finish, 0, p) for p in range(pieces)]
    spaced(main, relays)
    tokens_t[...] = rows_of(token_rows).T
    gathered(1)
    compute(1, 0)
    for p in range(1, pieces):
        compute(1, p)
        reduce_pair(1, p - 1)
    reduce_pair(1, pieces - 1)
    arrive(0)
    lead = [call(output, 0, 0)]
    for q in range(1, chunks):
        lead += [call(output, 0, q), call(reduce_near, 0, q - 1)]
    spaced(lead, [call(finish, 1, p) for p in range(pieces)])
    reduce_near(0, chunks - 1)
    act_t[...] = rows_of(act).T
    arrive(1)
    output(1, 0)
    for q in range(1, chunks):
        output(1, q)
        settle(0, q - 1)
        reduce_near(1, q - 1)
    settle(0, chunks - 1)
    reduce_near(1, chunks - 1)
    for q in range(chunks):
        settle(1, q)
    for copy in sent:
        copy.wait_send()


ANY = pl.BlockSpec(memory_space=pl.ANY)


def layer_stage(far, near, chips, cores, first, second, masks, down, up):
    depth, width = down.shape
    tokens = first.shape[0] * far * near
    cols, span = cut(width, COLS), cut(depth, SPAN)
    pieces, chunks = width // cols, depth // span
    half, share = tokens // cores, tokens // (far * near)
    full = (far * near,) + first.shape
    bf16, f32 = jnp.bfloat16, jnp.float32
    tokens_t, act_t, hid, grad_rows, mixed, tokens_grad = pl.pallas_call(
        functools.partial(layer_kernel, far, near, chips, cores),
        out_shape=(
            jax.ShapeDtypeStruct((depth, tokens), bf16), jax.ShapeDtypeStruct((width, tokens), bf16),
            jax.ShapeDtypeStruct((cores, half, width), bf16), jax.ShapeDtypeStruct(full, bf16),
            jax.ShapeDtypeStruct((share, depth), bf16), jax.ShapeDtypeStruct((share, depth), bf16),
        ),
        in_specs=[VMEM] * 4 + [ANY] * 2,
        out_specs=(VMEM,) * 6,
        scratch_shapes=[
            pltpu.VMEM((depth // BLK * SUB, width), bf16), pltpu.VMEM((width // BLK * SUB, depth), bf16),
            pltpu.VMEM((depth, width), bf16), pltpu.VMEM((width, depth), bf16), DMA((pieces,)), DMA((pieces,)),
            pltpu.VMEM(full, bf16), pltpu.VMEM((cores, half, width), bf16),
            DMA((2, far - 1)), DMA((2, far - 1)), DMA((2, far, near - 1)), DMA((2, far, near - 1)), DMA((2,)),
            pltpu.VMEM((2, pieces, cores, half, cols), f32), pltpu.VMEM((2, pieces, half, cols), f32),
            pltpu.VMEM((2, pieces, half, cols), bf16), pltpu.VMEM((2, pieces, chips - 1, half, cols), bf16),
            pltpu.VMEM((pieces, half, cols), f32),
            DMA((2, pieces)), DMA((2, pieces)),
            DMA((2, pieces, chips - 1)), DMA((2, pieces, chips - 1)),
            DMA((2, pieces)), DMA((2, pieces)),
            pltpu.VMEM((2, chunks, far, near, share, span), f32),
            pltpu.VMEM((2, chunks, far, near, share, span), bf16),
            pltpu.VMEM((2, chunks, near - 1, far, share, span), bf16),
            pltpu.VMEM((2, chunks, far - 1, share, span), bf16),
            pltpu.VMEM((2, chunks, far - 1, share, span), bf16),
            DMA((2, chunks, near - 1)), DMA((2, chunks, near - 1)),
            DMA((2, chunks, far - 1)), DMA((2, chunks, far - 1)),
        ],
        compiler_params=pltpu.CompilerParams(
            collective_id=0, has_side_effects=True, vmem_limit_bytes=67043328
        ),
        name="layer_stage",
    )(first, second, *masks, down, up)
    flat = lambda each: each.reshape(tokens, each.shape[-1])
    return tokens_t, act_t, flat(hid), flat(grad_rows), mixed, tokens_grad


def outer_kernel(tokens_ref, hid_ref, in_mask, act_ref, grad_ref, out_mask, mixed_ref, back_ref, *outs):
    in_ref, out_ref, mixed_out, back_out = outs
    step = pl.program_id(0)

    @pl.when(step == 0)
    def _():
        mixed_out[...] = mixed_ref[...]
        back_out[...] = back_ref[...]

    def one(left, right, mask, out):
        count = out.shape[0] // BLK
        full = jnp.dot(left[...], right[...], preferred_element_type=jnp.float32)
        out[...] = masked(full.astype(out.dtype), spread(mask[...], step * count, count))

    one(tokens_ref, hid_ref, in_mask, in_ref)
    one(act_ref, grad_ref, out_mask, out_ref)


def outers(tokens, hid, in_mask, act, grad, out_mask, mixed, back):
    depth, count = tokens.shape
    width = hid.shape[1]
    steps = math.gcd(depth // BLK, width // BLK)
    while steps % 2 == 0 and depth // steps < STEP:
        steps //= 2
    down, up = depth // steps, width // steps
    whole = lambda each: pl.BlockSpec(each.shape, lambda i: (0, 0))
    same = lambda each: jax.ShapeDtypeStruct(each.shape, each.dtype)
    return pl.pallas_call(
        outer_kernel,
        grid=(steps,),
        out_shape=[
            jax.ShapeDtypeStruct((depth, width), jnp.bfloat16), jax.ShapeDtypeStruct((width, depth), jnp.bfloat16),
            same(mixed), same(back),
        ],
        in_specs=[
            pl.BlockSpec((down, count), lambda i: (i, 0)), whole(hid), whole(in_mask),
            pl.BlockSpec((up, count), lambda i: (i, 0)), whole(grad), whole(out_mask),
            whole(mixed), whole(back),
        ],
        out_specs=[
            pl.BlockSpec((down, width), lambda i: (i, 0)), pl.BlockSpec((up, depth), lambda i: (i, 0)),
            whole(mixed), whole(back),
        ],
        name="outers",
    )(tokens, hid, in_mask, act, grad, out_mask, mixed, back)


def local(far, near, chips, cores, tokens, w_in, w_out, mask_in, mask_out, out_grad):
    tokens_t, act_t, hid, grad_rows, mixed, tokens_grad = layer_stage(
        far, near, chips, cores, tokens, out_grad, (mask_in, mask_out), w_in, w_out
    )
    w_in_grad, w_out_grad, mixed, tokens_grad = outers(
        tokens_t, hid, mask_in, act_t, grad_rows, mask_out, mixed, tokens_grad
    )
    return (mixed, tokens_grad, w_in_grad, w_out_grad)


def solution(mesh):
    columns, rows = mesh.shape["col"], mesh.shape["row"]
    near = 2 ** (int(math.log2(columns)) // 2)
    return jax.shard_map(
        functools.partial(local, columns // near, near, rows // 2, 2),
        mesh=mesh,
        in_specs=(
            P("col", "row"),
            P("row", "col"),
            P("col", "row"),
            P("row", "col"),
            P("col", "row"),
            P("col", "row"),
        ),
        out_specs=(P("col", "row"), P("col", "row"), P("row", "col"), P("col", "row")),
        check_vma=False,
    )
```

time: 128 us -> 113 us (0.88); the launches traced: 127 us -> 113 us
  Pallas kernels: 123 us -> 113 us
  local copies, waits for them, and re-layouts: 3.08 us -> 0 us
    pallas_call x2 -> x1, Pallas kernels: 105 us -> 89.7 us  [layer_stage(): pl.pallas_call(functools.partial(layer_kernel, far, near, chips, cores),...]
    pallas_call x1, Pallas kernels: 18.3 us -> 22.9 us  [outers(): pl.pallas_call(outer_kernel, grid=(steps,), out_shape=[jax.ShapeDtypeStru...]
    unnamed x2 -> x0, local copies, waits for them, and re-layouts: 3.08 us -> none
where the time goes in v1:
time: 113 us
  Pallas kernels  113 us (100%)
    pallas_call x1, Pallas kernels, layer_stage(): pl.pallas_call(functools.partial(layer_kernel, far, near, chips, cores),...  89.7 us
    pallas_call x1, Pallas kernels, outers(): pl.pallas_call(outer_kernel, grid=(steps,), out_shape=[jax.ShapeDtypeStru...  22.9 us

profile of v1, /device:TPU:0, one launch (start us, length us, event | category | flops | bytes accessed | tf_op | source)
XLA Modules:
  0.0 113.2 jit_solution(12409110667898363750)
XLA Ops:
  0.6 89.7 %layer_stage.1 = (bf16[3072,128]{1,0:T(8,128)(2,1)}, bf16[3072,128]{1,0:T(8,128)(2,1)}, bf16[2,64,3072]{2,1,0:T(8,128)(2,1)}, bf16[8,16,3072]{2,1,0:T(8,128)(2,1...) custom-call(bf16[16,3072]{1,0:T(8,128)(2,1)} %refs_0_.1, bf16[16,3072]{1,0:T(8,128)(2,1)} %refs_1_.1, ...), custom_call_target="tpu_custom_call" | custom-call | tf_op jit(solution)/shard_map/layer_stage/pallas_call | solution.py:280
  90.3 22.9 %outers.1 = (bf16[3072,3072]{1,0:T(8,128)(2,1)}, bf16[3072,3072]{1,0:T(8,128)(2,1)}, bf16[16,3072]{1,0:T(8,128)(2,1)}, bf16[16,3072]{1,0:T(8,128)(2,1)}) custom-call(bf16[3072,128]{1,0:T(8,128)(2,1)} %get-tuple-element.14.tokens_ref, bf16[128,3072]{1,0:T(8,128)(2,1)} %bitcast.2, s32[24,24]{1,0:T(8,128)} %in_mask.1, ...), custom_call_target="tpu_custom_call" | custom-call | tf_op jit(solution)/shard_map/outers/pallas_call | solution.py:344

commit v2 on v1

--- a/solution.py
+++ b/solution.py
@@ -12,6 +12,7 @@
 SUB = 16
 MESH = pl.DeviceIdType.MESH
 VMEM = pl.BlockSpec(memory_space=pltpu.VMEM)
+SMEM = pl.BlockSpec(memory_space=pltpu.SMEM)
 DMA = pltpu.SemaphoreType.DMA
 COLS, SPAN, STEP = 512, 512, 512
 GELU_A, GELU_B = 0.7978845608028654, 0.044715
@@ -24,18 +25,16 @@
     )
 
 
-def spread(mask, start, count):
+def spread(mask):
     rows, cols = mask.shape
 
-    def repeats(shape, dim, size, offset):
-        apart = lax.broadcasted_iota(jnp.int32, shape, dim) - size * (
-            lax.broadcasted_iota(jnp.int32, shape, 1 - dim) - offset
-        )
+    def repeats(shape, dim, size):
+        apart = lax.broadcasted_iota(jnp.int32, shape, dim) - size * lax.broadcasted_iota(jnp.int32, shape, 1 - dim)
         return jnp.where((apart >= 0) & (apart < size), 1.0, 0.0).astype(jnp.bfloat16)
 
     flags = mask.astype(jnp.float32).astype(jnp.bfloat16)
-    tall = jnp.dot(repeats((count * SUB, rows), 0, SUB, start), flags, preferred_element_type=jnp.float32)
-    wide = jnp.dot(tall.astype(jnp.bfloat16), repeats((cols, cols * BLK), 1, BLK, 0), preferred_element_type=jnp.float32)
+    tall = jnp.dot(repeats((rows * SUB, rows), 0, SUB), flags, preferred_element_type=jnp.float32)
+    wide = jnp.dot(tall.astype(jnp.bfloat16), repeats((cols, cols * BLK), 1, BLK), preferred_element_type=jnp.float32)
     return wide.astype(jnp.bfloat16)
 
 
@@ -100,9 +99,11 @@
             pl.semaphore_signal(barrier, inc=1, device_id={axis: peer}, device_id_type=MESH)
     pl.semaphore_wait(barrier, len(along_z) + len(along_y) + len(peers) + 1)
 
-    def give(a):
+    def near_give(a):
         for e, peer in enumerate(along_y):
             push(remote(srcs[a], dsts[a].at[mine], ys.at[a, 0, e], yr.at[a, 0, e], "col", peer))
+
+    def far_give(a):
         for d, peer in enumerate(along_z):
             push(remote(srcs[a], dsts[a].at[mine], zs.at[a, d], zr.at[a, d], "col", peer))
 
@@ -208,60 +209,59 @@
             total = total + far_parts[a, q, d].astype(jnp.float32)
         results[a][:, pl.ds(q * span, span)] = total.astype(results[a].dtype)
 
-    give(0)
+    near_give(0)
+    far_give(0)
     kept = [pltpu.make_async_copy(srcs[a], dsts[a].at[mine], own.at[a]) for a in range(2)]
     for copy in kept:
         copy.start()
+    far_give(1)
     for a in range(2):
-        flags[a][...] = spread(masks[a][...], 0, masks[a].shape[0])
+        flags[a][...] = spread(masks[a][...])
     for d in range(far - 1):
         relay(0, d)
-    give(1)
+    near_give(1)
     for p in range(pieces):
         load(1, p).start()
     gathered(0)
 
-    def spaced(main, side):
-        done = 0
+    def run(jobs):
+        for job in jobs:
+            job()
+
+    def merge(main, side, lag):
+        side = list(side)
         for n, job in enumerate(main):
             job()
-            upto = (n + 1) * len(side) // len(main)
-            for other in side[done:upto]:
-                other()
-            done = upto
+            if n >= lag and side:
+                side.pop(0)()
+        run(side)
+
+    def turn(out, ref):
+        out[...] = rows_of(ref).T
 
     call = functools.partial
-    relays = [call(relay, 1, d) for d in range(far - 1)]
-    main = [call(compute, 0, 0)]
+    each = lambda job, a, count: [call(job, a, n) for n in range(count)]
+    ends0, ends1 = each(finish, 0, pieces), each(finish, 1, pieces)
+    outs0, outs1 = each(output, 0, chunks), each(output, 1, chunks)
+    nears0, nears1 = each(reduce_near, 0, chunks), each(reduce_near, 1, chunks)
+    held_back = min(2, pieces - 1)
+    merge(each(compute, 0, pieces), each(reduce_pair, 0, pieces), 2)
+    run([call(relay, 1, d) for d in range(far - 1)])
+    turn(tokens_t, token_rows)
+    run(ends0[:pieces - held_back])
+    gathered(1)
+    turns = [call(compute, 1, 0)]
     for p in range(1, pieces):
-        main += [call(compute, 0, p), call(reduce_pair, 0, p - 1)]
-    main += [call(reduce_pair, 0, pieces - 1)]
-    main += [call(finish, 0, p) for p in range(pieces)]
-    spaced(main, relays)
-    tokens_t[...] = rows_of(token_rows).T
-    gathered(1)
-    compute(1, 0)
-    for p in range(1, pieces):
-        compute(1, p)
-        reduce_pair(1, p - 1)
-    reduce_pair(1, pieces - 1)
+        turns += [call(compute, 1, p), call(reduce_pair, 1, p - 1)]
+    merge(turns + [call(reduce_pair, 1, pieces - 1)], ends0[pieces - held_back:], 3)
     arrive(0)
-    lead = [call(output, 0, 0)]
-    for q in range(1, chunks):
-        lead += [call(output, 0, q), call(reduce_near, 0, q - 1)]
-    spaced(lead, [call(finish, 1, p) for p in range(pieces)])
-    reduce_near(0, chunks - 1)
-    act_t[...] = rows_of(act).T
+    merge(outs0, ends1[:pieces - held_back], 0)
+    merge(ends1[pieces - held_back:], nears0[:held_back], 0)
+    turn(act_t, act)
     arrive(1)
-    output(1, 0)
-    for q in range(1, chunks):
-        output(1, q)
-        settle(0, q - 1)
-        reduce_near(1, q - 1)
-    settle(0, chunks - 1)
-    reduce_near(1, chunks - 1)
-    for q in range(chunks):
-        settle(1, q)
+    merge(outs1, nears0[held_back:], 1)
+    merge(nears1, each(settle, 0, chunks), 0)
+    run(each(settle, 1, chunks))
     for copy in sent:
         copy.wait_send()
 
@@ -324,9 +324,12 @@
         back_out[...] = back_ref[...]
 
     def one(left, right, mask, out):
-        count = out.shape[0] // BLK
+        down, across = out.shape[0] // BLK, out.shape[1] // BLK
         full = jnp.dot(left[...], right[...], preferred_element_type=jnp.float32)
-        out[...] = masked(full.astype(out.dtype), spread(mask[...], step * count, count))
+        for b in range(down):
+            for c in range(across):
+                block = slice(b * BLK, (b + 1) * BLK), slice(c * BLK, (c + 1) * BLK)
+                out[block] = (full[block] * mask[step * down + b, c].astype(jnp.float32)).astype(out.dtype)
 
     one(tokens_ref, hid_ref, in_mask, in_ref)
     one(act_ref, grad_ref, out_mask, out_ref)
@@ -349,8 +352,8 @@
             same(mixed), same(back),
         ],
         in_specs=[
-            pl.BlockSpec((down, count), lambda i: (i, 0)), whole(hid), whole(in_mask),
-            pl.BlockSpec((up, count), lambda i: (i, 0)), whole(grad), whole(out_mask),
+            pl.BlockSpec((down, count), lambda i: (i, 0)), whole(hid), SMEM,
+            pl.BlockSpec((up, count), lambda i: (i, 0)), whole(grad), SMEM,
             whole(mixed), whole(back),
         ],
         out_specs=[

time: 113 us -> 98.8 us (0.87)
  Pallas kernels: 113 us -> 98 us
    pallas_call x1, Pallas kernels: 89.7 us -> 81.4 us  [layer_stage(): pl.pallas_call(functools.partial(layer_kernel, far, near, chips, cores),...]
    pallas_call x1, Pallas kernels: 22.9 us -> 16.6 us  [outers(): pl.pallas_call(outer_kernel, grid=(steps,), out_shape=[jax.ShapeDtypeStru...]
where the time goes in v2:
time: 98.8 us; the launch traced here: 98.7 us
  Pallas kernels  98 us (99%)
    pallas_call x1, Pallas kernels, layer_stage(): pl.pallas_call(functools.partial(layer_kernel, far, near, chips, cores),...  81.4 us
    pallas_call x1, Pallas kernels, outers(): pl.pallas_call(outer_kernel, grid=(steps,), out_shape=[jax.ShapeDtypeStru...  16.6 us

profile of v2, /device:TPU:0, one launch (start us, length us, event | category | flops | bytes accessed | tf_op | source)
XLA Modules:
  0.0 98.7 jit_solution(15030589753558204066)
XLA Ops:
  0.6 81.4 %layer_stage.1 = (bf16[3072,128]{1,0:T(8,128)(2,1)}, bf16[3072,128]{1,0:T(8,128)(2,1)}, bf16[2,64,3072]{2,1,0:T(8,128)(2,1)}, bf16[8,16,3072]{2,1,0:T(8,128)(2,1...) custom-call(bf16[16,3072]{1,0:T(8,128)(2,1)} %refs_0_.1, bf16[16,3072]{1,0:T(8,128)(2,1)} %refs_1_.1, ...), custom_call_target="tpu_custom_call" | custom-call | tf_op jit(solution)/shard_map/layer_stage/pallas_call | solution.py:280
  82.1 16.6 %outers.1 = (bf16[3072,3072]{1,0:T(8,128)(2,1)}, bf16[3072,3072]{1,0:T(8,128)(2,1)}, bf16[16,3072]{1,0:T(8,128)(2,1)}, bf16[16,3072]{1,0:T(8,128)(2,1)}) custom-call(bf16[3072,128]{1,0:T(8,128)(2,1)} %get-tuple-element.14.tokens_ref, bf16[128,3072]{1,0:T(8,128)(2,1)} %bitcast.2, s32[24,24]{1,0:T(8,128)} %in_mask.1, ...), custom_call_target="tpu_custom_call" | custom-call | tf_op jit(solution)/shard_map/outers/pallas_call | solution.py:347

commit v3 on v2

--- a/solution.py
+++ b/solution.py
@@ -58,8 +58,10 @@
 
 
 def layer_kernel(far, near, chips, cores, *refs):
-    srcs, masks, weights = refs[:2], refs[2:4], refs[4:6]
-    tokens_t, act_t, hid, grad_rows, mixed, tokens_grad = refs[6:12]
+    srcs, mask_refs, weights = refs[:2], refs[2:4], refs[4:6]
+    tokens_out, act_out, hid_out, grad_out, mixed, tokens_grad = refs[6:12]
+    refs, extra = refs[:-8], refs[-8:]
+    tokens_t, act_t, hid, grad_rows, *masks, read, saved = extra
     flags, held, loaded, token_rows, act = refs[12:14], refs[14:16], refs[16:18], refs[18], refs[19]
     zs, zr, ys, yr, own = refs[20:25]
     parts, pair, sums, landed, slopes, ps, pr, xs, xr, gs, gr = refs[25:36]
@@ -91,6 +93,9 @@
             return pltpu.make_async_copy(weights[0].at[:, spot], held[0].at[:, spot], loaded[0].at[p])
         return pltpu.make_async_copy(weights[1].at[spot, :], held[1].at[spot, :], loaded[1].at[p])
 
+    reads = [pltpu.make_async_copy(mask_refs[a], masks[a], read.at[a]) for a in range(2)]
+    for copy in reads:
+        copy.start()
     for p in range(pieces):
         load(0, p).start()
     barrier = pltpu.get_barrier_semaphore()
@@ -211,15 +216,16 @@
 
     near_give(0)
     far_give(0)
+    near_give(1)
     kept = [pltpu.make_async_copy(srcs[a], dsts[a].at[mine], own.at[a]) for a in range(2)]
     for copy in kept:
         copy.start()
     far_give(1)
     for a in range(2):
+        reads[a].wait()
         flags[a][...] = spread(masks[a][...])
     for d in range(far - 1):
         relay(0, d)
-    near_give(1)
     for p in range(pieces):
         load(1, p).start()
     gathered(0)
@@ -236,8 +242,14 @@
                 side.pop(0)()
         run(side)
 
-    def turn(out, ref):
-        out[...] = rows_of(ref).T
+    stored = [
+        pltpu.make_async_copy(own_ref, out, saved.at[n])
+        for n, (own_ref, out) in enumerate(((act_t, act_out), (hid, hid_out), (tokens_t, tokens_out), (grad_rows, grad_out)))
+    ]
+
+    def keep(n, turned, ref):
+        turned[...] = rows_of(ref).T
+        stored[n].start()
 
     call = functools.partial
     each = lambda job, a, count: [call(job, a, n) for n in range(count)]
@@ -245,23 +257,34 @@
     outs0, outs1 = each(output, 0, chunks), each(output, 1, chunks)
     nears0, nears1 = each(reduce_near, 0, chunks), each(reduce_near, 1, chunks)
     held_back = min(2, pieces - 1)
-    merge(each(compute, 0, pieces), each(reduce_pair, 0, pieces), 2)
-    run([call(relay, 1, d) for d in range(far - 1)])
-    turn(tokens_t, token_rows)
+    relay(1, 0)
+    rest = [call(relay, 1, d) for d in range(1, far - 1)]
+    turns = []
+    for p in range(pieces):
+        turns += [call(compute, 0, p)] + [call(reduce_pair, 0, p - 2)] * (p > 1)
+    turns += [call(reduce_pair, 0, p) for p in range(max(0, pieces - 2), pieces)]
+    merge(turns, rest[:-1], pieces)
+    run(rest[-1:])
+    keep(2, tokens_t, token_rows)
     run(ends0[:pieces - held_back])
     gathered(1)
+    stored[3].start()
     turns = [call(compute, 1, 0)]
     for p in range(1, pieces):
         turns += [call(compute, 1, p), call(reduce_pair, 1, p - 1)]
     merge(turns + [call(reduce_pair, 1, pieces - 1)], ends0[pieces - held_back:], 3)
     arrive(0)
     merge(outs0, ends1[:pieces - held_back], 0)
-    merge(ends1[pieces - held_back:], nears0[:held_back], 0)
-    turn(act_t, act)
+    keep(0, act_t, act)
+    early = max(1, chunks - 2)
+    merge(nears0[:early], ends1[pieces - held_back:], 0)
     arrive(1)
-    merge(outs1, nears0[held_back:], 1)
+    stored[1].start()
+    merge(outs1, nears0[early:], 1)
     merge(nears1, each(settle, 0, chunks), 0)
     run(each(settle, 1, chunks))
+    for copy in stored:
+        copy.wait()
     for copy in sent:
         copy.wait_send()
 
@@ -284,8 +307,8 @@
             jax.ShapeDtypeStruct((cores, half, width), bf16), jax.ShapeDtypeStruct(full, bf16),
             jax.ShapeDtypeStruct((share, depth), bf16), jax.ShapeDtypeStruct((share, depth), bf16),
         ),
-        in_specs=[VMEM] * 4 + [ANY] * 2,
-        out_specs=(VMEM,) * 6,
+        in_specs=[ANY] * 6,
+        out_specs=(ANY,) * 4 + (VMEM,) * 2,
         scratch_shapes=[
             pltpu.VMEM((depth // BLK * SUB, width), bf16), pltpu.VMEM((width // BLK * SUB, depth), bf16),
             pltpu.VMEM((depth, width), bf16), pltpu.VMEM((width, depth), bf16), DMA((pieces,)), DMA((pieces,)),
@@ -304,6 +327,10 @@
             pltpu.VMEM((2, chunks, far - 1, share, span), bf16),
             DMA((2, chunks, near - 1)), DMA((2, chunks, near - 1)),
             DMA((2, chunks, far - 1)), DMA((2, chunks, far - 1)),
+            pltpu.VMEM((depth, tokens), bf16), pltpu.VMEM((width, tokens), bf16),
+            pltpu.VMEM((cores, half, width), bf16), pltpu.VMEM(full, bf16),
+            pltpu.VMEM(masks[0].shape, masks[0].dtype), pltpu.VMEM(masks[1].shape, masks[1].dtype),
+            DMA((2,)), DMA((4,)),
         ],
         compiler_params=pltpu.CompilerParams(
             collective_id=0, has_side_effects=True, vmem_limit_bytes=67043328

time: 98.8 us -> 96.2 us (0.974)
  Pallas kernels: 98 us -> 95.4 us
    pallas_call x1, Pallas kernels: 81.4 us -> 78.8 us  [layer_stage(): pl.pallas_call(functools.partial(layer_kernel, far, near, chips, cores),...]
where the time goes in v3:
time: 96.2 us; the launch traced here: 96 us
  Pallas kernels  95.4 us (99%)
    pallas_call x1, Pallas kernels, layer_stage(): pl.pallas_call(functools.partial(layer_kernel, far, near, chips, cores),...  78.8 us
    pallas_call x1, Pallas kernels, outers(): pl.pallas_call(outer_kernel, grid=(steps,), out_shape=[jax.ShapeDtypeStru...  16.6 us

profile of v3, /device:TPU:0, one launch (start us, length us, event | category | flops | bytes accessed | tf_op | source)
XLA Modules:
  0.0 96.0 jit_solution(14603987766505109263)
XLA Ops:
  0.6 78.8 %layer_stage.1 = (bf16[3072,128]{1,0:T(8,128)(2,1)}, bf16[3072,128]{1,0:T(8,128)(2,1)}, bf16[2,64,3072]{2,1,0:T(8,128)(2,1)}, bf16[8,16,3072]{2,1,0:T(8,128)(2,1...) custom-call(bf16[16,3072]{1,0:T(8,128)(2,1)} %refs_0_.1, bf16[16,3072]{1,0:T(8,128)(2,1)} %refs_1_.1, ...), custom_call_target="tpu_custom_call" | custom-call | tf_op jit(solution)/shard_map/layer_stage/pallas_call | solution.py:303
  79.4 16.6 %outers.1 = (bf16[3072,3072]{1,0:T(8,128)(2,1)}, bf16[3072,3072]{1,0:T(8,128)(2,1)}, bf16[16,3072]{1,0:T(8,128)(2,1)}, bf16[16,3072]{1,0:T(8,128)(2,1)}) custom-call(bf16[3072,128]{1,0:T(8,128)(2,1)} %get-tuple-element.14.tokens_ref, bf16[128,3072]{1,0:T(8,128)(2,1)} %bitcast.2, s32[24,24]{1,0:T(8,128)} %in_mask.1, ...), custom_call_target="tpu_custom_call" | custom-call | tf_op jit(solution)/shard_map/outers/pallas_call | solution.py:374
